TPU v7x, 128 devices: a whole 4x4x4 slice. The times are simulated.
128 devices in a mesh: gx: 8 (over x, core), gy: 4 (over z), band: 4 (over y).
Axes of the slice: x: 4, y: 4, z: 4, core: 2. Of those that a mesh axis runs over, the one named last changes fastest.
Arguments:
- block: float32 [32, 96, 18432], P('band', 'gx', 'gy'), may hold values from -9 to 9
- prior: float32 [256, 96, 18432], P('band', 'gx', 'gy'), may hold values from -9 to 9
- potential: float32 [96, 18432], P('gx', 'gy'), may hold values from -1.5 to 1
Outputs:
- orbitals: float32 [32, 96, 18432], P('band', 'gx', 'gy')
All inputs are finite; a program needn't handle non-finite values.
Results may differ from a plain program's by a relative error of at most 0.000098.
Values sent between devices are 32-bit elements; how exact they have to be, the bound alone decides.
A program may use at most 128 MiB of HBM per device.

v0:
```python
import jax
import jax.numpy as jnp
from jax import lax
from jax.sharding import PartitionSpec as P

NZ = 192


coeffs = (-205.0 / 72.0, 8.0 / 5.0, -1.0 / 5.0, 8.0 / 315.0, -1.0 / 560.0)


def extended_2(x, sides, width):
    for axis, dim in sides:
        devices, length = (lax.axis_size(axis), x.shape[dim])
        up = [(i, (i + 1) % devices) for i in range(devices - 1)]
        down = [(j, i) for i, j in up]
        last = lax.slice_in_dim(x, length - width, length, axis=dim)
        leading = lax.slice_in_dim(x, 0, width, axis=dim)
        before = lax.ppermute(last, axis, up)
        after = lax.ppermute(leading, axis, down)
        x = jnp.concatenate([before, x, after], axis=dim)
    return x


def laplace(padded):
    center = padded[:, 4:-4, 4:-4, 4:-4]
    total = 3.0 * coeffs[0] * center
    for shift in range(1, 5):
        total = total + coeffs[shift] * (
            padded[:, 4 + shift : padded.shape[1] - 4 + shift, 4:-4, 4:-4]
            + padded[:, 4 - shift : padded.shape[1] - 4 - shift, 4:-4, 4:-4]
        )
        total = total + coeffs[shift] * (
            padded[:, 4:-4, 4 + shift : padded.shape[2] - 4 + shift, 4:-4]
            + padded[:, 4:-4, 4 - shift : padded.shape[2] - 4 - shift, 4:-4]
        )
        total = total + coeffs[shift] * (
            padded[:, 4:-4, 4:-4, 4 + shift : padded.shape[3] - 4 + shift]
            + padded[:, 4:-4, 4:-4, 4 - shift : padded.shape[3] - 4 - shift]
        )
    return total


def matmul(left, right):
    return jnp.dot(left, right, precision=lax.Precision.HIGHEST, preferred_element_type=jnp.float32)


def shards(block, prior, potential):
    own_count = block.shape[0]
    rows_x = block.shape[1]
    rows_y = block.shape[2] // NZ
    total_count = own_count * lax.axis_size("band")
    ncells_all = rows_x * lax.axis_size("gx") * rows_y * lax.axis_size("gy") * NZ
    grid_block = block.reshape(own_count, rows_x, rows_y, NZ)
    extended = extended_2(grid_block, (("gx", 1), ("gy", 2)), 4)
    extended = jnp.pad(extended, ((0, 0), (0, 0), (0, 0), (4, 4)))
    lap_flat = laplace(extended).reshape(block.shape)
    phi = -2.0 * lap_flat + potential[None] * block
    phi_flat = phi.reshape(own_count, -1)
    prior_flat = prior.reshape(prior.shape[0], -1)
    phi_all = lax.all_gather(phi_flat, "band", axis=0, tiled=True)
    correlation = lax.psum(matmul(prior_flat, phi_all.T), ("gx", "gy")) / ncells_all
    removed = lax.psum_scatter(
        matmul(correlation.T, prior_flat), "band", scatter_dimension=0, tiled=True
    )
    projected_own = phi_flat - removed
    projected = lax.all_gather(projected_own, "band", axis=0, tiled=True)
    gram = lax.psum(matmul(projected, projected.T), ("gx", "gy")) / ncells_all
    lower = jnp.linalg.cholesky(gram)
    inverse = lax.linalg.triangular_solve(
        lower, jnp.eye(total_count, dtype=lower.dtype), left_side=True, lower=True
    )
    first_row = lax.axis_index("band") * own_count
    own_rows = lax.dynamic_slice_in_dim(inverse, first_row, own_count, 0)
    orbitals = matmul(own_rows, projected)
    return orbitals.reshape(block.shape)


def solution(mesh):
    in_specs = (P("band", "gx", "gy"), P("band", "gx", "gy"), P("gx", "gy"))
    out_specs = P("band", "gx", "gy")
    return jax.shard_map(shards, mesh=mesh, in_specs=in_specs, out_specs=out_specs, check_vma=False)
```

profile of v0, /device:TPU:0, one launch (start us, length us, event | category | flops | bytes accessed | tf_op | source)
XLA Modules:
  0.0 602.9 jit_solution(7956143481172874915)
XLA Ops:
  6.5 2.0 reshape.25
  8.7 1.3 collective-permute-start.1
  10.0 1.3 collective-permute-start
  11.3 0.5 collective-permute-done.1
  12.0 0.8 constant_dynamic-update-slice_fusion.1
  12.9 3.1 collective-permute-done
  16.1 0.3 fusion.47
  16.4 1.3 collective-permute-start.2
  17.7 4.6 collective-permute-start.3
  22.3 6.6 %collective-permute-done.2 = f32[8,20,4,192]{3,2,0,1:T(4,128)S(1)} collective-permute-done((f32[8,20,4,192]{3,2,0,1:T(4,128)S(1)}, f32[8,20,4,192]{3,2,0,1:T(4,128)S(1)}, u32[]{:S(2)}, u32[]{:S(2)}) %collective-permute-start.2) | collective-permute-done | bytes 491552 | tf_op jit(solution)/shard_map/ppermute | solution.py:20
  28.9 1.5 collective-permute-done.3
  30.3 2.9 select_maximum_fusion
  33.2 20.7 %fusion.9 = f32[8,12,24,192]{3,2,0,1:T(8,128)} fusion(f32[8,20,24,192]{3,2,0,1:T(8,128)} %copy-done.3, f32[8,20,4,192]{3,2,0,1:T(4,128)S(1)} %collective-permute-done.3, f32[8,20,4,192]{3,2,0,1:T(4,128)S(1)} %collective-permute-done.2, f32[8,20,32,200]{3,2,0,1:T(8,128)S(1)} %select_maximum_fusion, f32[8,16,24,192]{3,2,0,1:T(8,128)} %copy-done.1, ...), kind=kLoop, calls=%fused_computation.25 | loop fusion | flops 20348928 | bytes 35782656 | tf_op jit(solution)/shard_map/mul | solution.py:58
  53.9 2.3 mul.78
  56.2 2.4 multiply_add_fusion
  58.7 0.2 reduce-scatter.2.cloned.1.call-start
  58.9 11.4 %copy.10 = f32[12,8,8,4608]{3,2,0,1:T(8,128)} copy(f32[12,8,8,4608]{3,2,1,0:T(8,128)} %bitcast.31) | data formatting | bytes 28311552 | tf_op jit(solution)/shard_map/reshape | solution.py:60
  70.3 79.2 %all-gather.3.cloned.1.call-done = f32[32,55296]{1,0:T(8,128)} async-done(((f32[8,55296]{1,0:T(8,128)}), f32[32,55296]{1,0:T(8,128)}) %all-gather.3.cloned.1.call-update) | async-done | bytes 7077904 | tf_op jit(solution)/shard_map/all_gather | solution.py:61
  149.5 14.5 %convolution_bitcast_fusion = f32[64,32]{0,1:T(8,128)S(1)} fusion(f32[32,55296]{1,0:T(8,128)} %all-gather.3.cloned.1.call-done, f32[64,55296]{1,0:T(8,128)} %bitcast.27), kind=kOutput, calls=%fused_computation.63 | convolution fusion | flops 1358954496 | bytes 21241856 | tf_op jit(solution)/shard_map/dot_general | solution.py:45
  164.0 128.3 %psum.14 = f32[64,32]{0,1:T(8,128)S(1)} all-reduce(f32[64,32]{0,1:T(8,128)S(1)} %convolution_bitcast_fusion), channel_id=1, replica_groups=mesh['gx'=8,'gy'=4,'band'=4] {'gx','gy'}, use_global_device_ids=true, to_apply=%region_0.1 | all-reduce | flops 2048 | bytes 16384 | tf_op jit(solution)/shard_map/psum | solution.py:62
  292.3 11.7 %fusion.40 = f32[32,55296]{1,0:T(8,128)} fusion(f32[64,55296]{1,0:T(8,128)} %bitcast.28, f32[64,32]{0,1:T(8,128)S(1)} %psum.14), kind=kOutput, calls=%fused_computation.78 | convolution fusion | flops 1358956544 | bytes 21241856 | tf_op jit(solution)/shard_map/dot_general | solution.py:45
  304.0 66.2 %reduce-scatter.2.cloned.1.call-done = f32[8,55296]{1,0:T(8,128)} async-done(((f32[32,55296]{1,0:T(8,128)}), f32[8,55296]{1,0:T(8,128)}) %reduce-scatter.2.cloned.1.call-update) | async-done | bytes 1769488 | tf_op jit(solution)/shard_map/reduce_scatter | solution.py:63
  370.3 2.9 sub.3
  373.1 72.1 %all-gather.5.cloned.1.call-done = f32[32,55296]{1,0:T(8,128)} async-done(((f32[8,55296]{1,0:T(8,128)}), f32[32,55296]{1,0:T(8,128)}) %all-gather.5.cloned.1.call-update) | async-done | bytes 7077904 | tf_op jit(solution)/shard_map/all_gather | solution.py:67
  445.3 9.1 %fusion.49 = f32[32,32]{0,1:T(8,128)S(1)} fusion(f32[32,55296]{1,0:T(8,128)} %all-gather.5.cloned.1.call-done), kind=kOutput, calls=%fused_computation.91 | convolution fusion | flops 679477248 | bytes 7081984 | tf_op jit(solution)/shard_map/dot_general | solution.py:45
  454.4 128.5 %psum.15 = f32[32,32]{0,1:T(8,128)S(1)} all-reduce(f32[32,32]{0,1:T(8,128)S(1)} %fusion.49), channel_id=1, replica_groups=mesh['gx'=8,'gy'=4,'band'=4] {'gx','gy'}, use_global_device_ids=true, to_apply=%region_2.3 | all-reduce | flops 1024 | bytes 8192 | tf_op jit(solution)/shard_map/psum | solution.py:68
  583.0 2.9 cholesky.17
  585.9 0.6 compare_reduce_fusion
  586.6 0.7 fusion.36
  587.2 2.4 custom-call.6
  589.6 0.2 fusion.37
  589.9 6.5 %fusion.43 = f32[8,55296]{1,0:T(8,128)} fusion(f32[32,55296]{1,0:T(8,128)} %all-gather.5.cloned.1.call-done, f32[32,32]{1,0:T(8,128)S(1)} %fusion.37, s32[]{:T(128)S(6)} %select_n.8), kind=kOutput, calls=%fused_computation.84 | convolution fusion | flops 169869312 | bytes 8851460 | tf_op jit(solution)/shard_map/dot_general | solution.py:45
  (24 shorter events, 0.6 us)
Async XLA Ops:
  6.5 142.9 %all-gather.3.cloned.1.call-start = ((), (), s32[]{:S(2)}) async-start(), calls=%async_computation.1 | async-start | bytes 8847360 | tf_op jit(solution)/shard_map/all_gather | solution.py:61
  8.5 3.5 copy-start.2
  8.7 3.2 collective-permute-start.1
  10.0 5.9 collective-permute-start
  12.9 3.5 copy-start.1
  16.1 17.1 %copy-start = (f32[8,16,24,192]{3,2,0,1:T(8,128)}, f32[8,16,24,192]{3,2,0,1:T(8,128)S(1)}, u32[]{:S(2)}) copy-start(f32[8,16,24,192]{3,2,0,1:T(8,128)S(1)} %get-tuple-element.12) | copy-start | bytes 7077892
  16.1 17.1 %copy-start.3 = (f32[8,20,24,192]{3,2,0,1:T(8,128)}, f32[8,20,24,192]{3,2,0,1:T(8,128)S(1)}, u32[]{:S(2)}) copy-start(f32[8,20,24,192]{3,2,0,1:T(8,128)S(1)} %get-tuple-element.13) | copy-start | bytes 8847364
  16.4 12.5 %collective-permute-start.2 = (f32[8,20,4,192]{3,2,0,1:T(4,128)S(1)}, f32[8,20,4,192]{3,2,0,1:T(4,128)S(1)}, u32[]{:S(2)}, u32[]{:S(2)}) collective-permute-start(f32[8,20,4,192]{3,2,0,1:T(4,128)S(1)} %get-tuple-element.5), channel_id=1, source_target_pairs={{4,0},{8,4},{12,8},{5,1},{9,5},{13,9},{6,2},{10,6},{14,10},{7,3},{... | collective-permute-start | bytes 1474568 | tf_op jit(solution)/shard_map/ppermute | solution.py:20
  17.7 12.6 %collective-permute-start.3 = (f32[8,20,4,192]{3,2,0,1:T(4,128)S(1)}, f32[8,20,4,192]{3,2,0,1:T(4,128)S(1)}, u32[]{:S(2)}, u32[]{:S(2)}) collective-permute-start(f32[8,20,4,192]{3,2,0,1:T(4,128)S(1)} %get-tuple-element.6), channel_id=1, source_target_pairs={{0,4},{4,8},{8,12},{1,5},{5,9},{9,13},{2,6},{6,10},{10,14},{3,7},{... | collective-permute-start | bytes 1474568 | tf_op jit(solution)/shard_map/ppermute | solution.py:19
  53.9 2.3 copy-start.5
  58.7 311.6 %reduce-scatter.2.cloned.1.call-start = ((), (), s32[]{:S(2)}) async-start(), calls=%async_computation.2 | async-start | bytes 8847360 | tf_op jit(solution)/shard_map/reduce_scatter | solution.py:63
  304.0 66.3 %copy-start.4 = (f32[8,12,4608]{2,0,1:T(8,128)S(1)}, f32[8,12,4608]{2,0,1:T(8,128)}, u32[]{:S(2)}) copy-start(f32[8,12,4608]{2,0,1:T(8,128)} %multiply_add_fusion) | copy-start | bytes 5308420
  304.0 141.3 %all-gather.5.cloned.1.call-start = ((), (), s32[]{:S(2)}) async-start(), calls=%async_computation.3 | async-start | bytes 8847360 | tf_op jit(solution)/shard_map/all_gather | solution.py:67
Sparse Core Ops, SparseCore 0:
  58.8 90.6 all-gather.2
  304.1 66.1 reduce-scatter.1
  373.3 71.9 all-gather.4
where the time goes:
time: 603 us
  blocking collectives  257 us (43%)
  waiting for transfers between devices  229 us (38%)
  matrix products  42 us (7%)
  other arithmetic  35.5 us (6%)
  local copies, waits for them, and re-layouts  17.2 us (3%)
  between operations  13.3 us (2%)
  starting transfers between devices  8.78 us (1%)
    psum x1, blocking collectives, shards(): gram = lax.psum(matmul(projected, projected.T), ('gx', 'gy')) / ncells_all  129 us
    psum x1, blocking collectives, shards(): lax.psum(matmul(prior_flat, phi_all.T), ('gx', 'gy')) / ncells_all  128 us
    all_gather x1, waiting for transfers between devices, shards(): phi_all = lax.all_gather(phi_flat, 'band', axis=0, tiled=True)  79.2 us
    all_gather x1, waiting for transfers between devices, shards(): projected = lax.all_gather(projected_own, 'band', axis=0, tiled=True)  72.1 us
    reduce_scatter x1, waiting for transfers between devices, shards(): lax.psum_scatter(matmul(correlation.T, prior_flat), 'band', scatter_dimen...  66.2 us
    dot_general x4, matrix products, matmul(): jnp.dot(left, right, precision=lax.Precision.HIGHEST, preferred_element_t...  41.8 us
    mul x1, other arithmetic, shards(): phi = -2.0 * lap_flat + potential[None] * block  20.7 us
  transfers between devices with their start and end apart: 7, of which 7 were waited for; matrix products, arithmetic and copies ran while one was open for 2% of the time, Pallas kernels for 0%

commit v1 on v0

v1 whole, which is shorter than its diff:
```python
import functools

import jax
import jax.numpy as jnp
from jax import lax
from jax.experimental import pallas as pl
from jax.experimental.pallas import tpu as pltpu
from jax.sharding import PartitionSpec as P

NZ = 192
WIDTH = 4 * NZ
CHUNK = 2 * NZ
WIDE = 2 * CHUNK
F32 = jnp.float32
BF16 = jnp.bfloat16
MESH = pl.DeviceIdType.MESH

coeffs = (-205.0 / 72.0, 8.0 / 5.0, -1.0 / 5.0, 8.0 / 315.0, -1.0 / 560.0)


def halves(value):
    high = value.astype(BF16)
    low = (value - high.astype(F32)).astype(BF16)
    return jnp.concatenate([high, low], axis=0)


def dot(left, right):
    return jnp.dot(left, right, preferred_element_type=F32)


def dot_nt(left, right):
    return lax.dot_general(left, right, (((1,), (1,)), ((), ())), preferred_element_type=F32)


def remote(src, dst, send, recv, axis, peer):
    return pltpu.make_async_remote_copy(
        src_ref=src, dst_ref=dst, send_sem=send, recv_sem=recv, device_id={axis: peer}, device_id_type=MESH
    )


def all_reduce(value, stages, slots, send, recv):
    for at, axis, me, n in stages:
        slots[at, me] = value
        copies = []
        for k in range(1, n):
            copy = remote(
                slots.at[at, me], slots.at[at, me], send.at[at, k - 1], recv.at[at, k - 1], axis, lax.rem(me + k, n)
            )
            copy.start()
            copies.append(copy)
        for copy in copies:
            copy.wait()
        value = slots[at, 0]
        for k in range(1, n):
            value = value + slots[at, k]
    return value


def inverse_factor(gram):
    count = gram.shape[0]
    row = lax.broadcasted_iota(jnp.int32, gram.shape, 0)
    lane = lax.broadcasted_iota(jnp.int32, gram.shape, 1)
    table = jnp.where(lane < count, gram, jnp.where(lane - count == row, 1.0, 0.0))
    for k in range(count - 1):
        pivot = table[k : k + 1, :]
        factor = table[:, k : k + 1] / table[k : k + 1, k : k + 1]
        table = table - jnp.where(row > k, factor, 0.0) * pivot
    diagonal = jnp.sum(jnp.where(lane == row, table, 0.0), axis=1, keepdims=True)
    inverse = jnp.where((lane >= count) & (lane < 2 * count), table * (1.0 / jnp.sqrt(diagonal)), 0.0)
    return inverse + pltpu.roll(inverse, gram.shape[1] - count, axis=1)


def kernel(
    sizes, ncells, block, prior, potential, out,
    grid, phi, staged, stacked, product, opposite, sides, opposite_in, sides_in, projected, pieces, result, slots,
    local_sem, stage_sem, halo_send, halo_recv, ring_send, ring_recv, relay_send, relay_recv,
    opp_send, opp_recv, side_send, side_recv, sum_send, sum_recv, back_send, back_recv,
):
    nx, ny, nb = sizes
    gx, gy, band = lax.axis_index("gx"), lax.axis_index("gy"), lax.axis_index("band")
    planes, own, cells = block.shape
    quarter = planes // nb
    count = nb * own
    right, left, across = lax.rem(band + 1, nb), lax.rem(band + nb - 1, nb), lax.rem(band + 2, nb)

    fill = pltpu.make_async_copy(block, grid.at[pl.ds(4, planes), :, pl.ds(WIDTH, cells)], local_sem.at[0])
    fill.start()

    def stage(x, slot):
        return pltpu.make_async_copy(prior.at[x], staged.at[slot], stage_sem.at[slot])

    stage(0, 0).start()
    stage(1, 1).start()

    barrier = pltpu.get_barrier_semaphore()
    for axis, me, n in (("gx", gx, nx), ("gy", gy, ny), ("band", band, nb)):
        for k in range(1, n):
            pl.semaphore_signal(barrier, inc=1, device_id={axis: lax.rem(me + k, n)}, device_id_type=MESH)
    pl.semaphore_wait(barrier, nx + ny + nb - 3)

    middle = pl.ds(WIDTH, cells)
    inner = pl.ds(4, planes)
    halos = (
        (0, "gx", gx, nx, 1, block.at[pl.ds(planes - 4, 4)], grid.at[pl.ds(0, 4), :, middle]),
        (1, "gx", gx, nx, -1, block.at[pl.ds(0, 4)], grid.at[pl.ds(planes + 4, 4), :, middle]),
        (2, "gy", gy, ny, 1, block.at[:, :, pl.ds(cells - WIDTH, WIDTH)], grid.at[inner, :, pl.ds(0, WIDTH)]),
        (3, "gy", gy, ny, -1, block.at[:, :, pl.ds(0, WIDTH)], grid.at[inner, :, pl.ds(WIDTH + cells, WIDTH)]),
    )

    def halo(at, axis, me, n, step, src, dst):
        copy = remote(src, dst, halo_send.at[at], halo_recv.at[at], axis, lax.rem(me + step + n, n))
        sends, receives = (me < n - 1, me > 0) if step == 1 else (me > 0, me < n - 1)
        return copy, sends, receives, dst

    for entry in halos:
        copy, sends, receives, dst = halo(*entry)
        pl.when(sends)(copy.start)

    for entry in halos:
        copy, sends, receives, dst = halo(*entry)

        @pl.when(jnp.logical_not(receives))
        def _(dst=dst):
            dst[...] = jnp.zeros(dst.shape, F32)

    fill.wait()
    for entry in halos:
        copy, sends, receives, dst = halo(*entry)
        pl.when(receives)(copy.wait_recv)
        pl.when(sends)(copy.wait_send)

    depth = lax.rem(lax.broadcasted_iota(jnp.int32, (own, CHUNK), 1), NZ)
    ups = [jnp.where(depth < NZ - m, coeffs[m], 0.0).astype(F32) for m in range(1, 5)]
    downs = [jnp.where(depth >= m, coeffs[m], 0.0).astype(F32) for m in range(1, 5)]

    def to_right(x):
        return remote(phi.at[x, band], phi.at[x, band], ring_send.at[0, x], ring_recv.at[0, x], "band", right)

    def to_left(x):
        return remote(phi.at[x, band], phi.at[x, band], ring_send.at[1, x], ring_recv.at[1, x], "band", left)

    def hamiltonian(x, carry):
        for start in range(0, cells, CHUNK):
            s = WIDTH + start
            center = grid[x + 4, :, pl.ds(s, CHUNK)]
            total = 3.0 * coeffs[0] * center
            for m in range(1, 5):
                total = total + coeffs[m] * (
                    grid[x + 4 + m, :, pl.ds(s, CHUNK)] + grid[x + 4 - m, :, pl.ds(s, CHUNK)]
                )
            for m in (2, 4):
                total = total + coeffs[m] * (
                    grid[x + 4, :, pl.ds(s + m * NZ, CHUNK)] + grid[x + 4, :, pl.ds(s - m * NZ, CHUNK)]
                )
            odd = None
            for m in (1, 3):
                term = coeffs[m] * (
                    grid[x + 4, :, pl.ds(s + m * NZ - 64, CHUNK + 128)]
                    + grid[x + 4, :, pl.ds(s - m * NZ - 64, CHUNK + 128)]
                )
                odd = term if odd is None else odd + term
            total = total + pltpu.roll(odd, CHUNK + 64, axis=1)[:, :CHUNK]
            for m in range(1, 5):
                total = total + ups[m - 1] * pltpu.roll(center, CHUNK - m, axis=1)
                total = total + downs[m - 1] * pltpu.roll(center, m, axis=1)
            weight = potential[pl.ds(x, 1), pl.ds(start, CHUNK)]
            phi[x, band, :, pl.ds(start, CHUNK)] = weight * center - 2.0 * total
        to_right(x).start()
        to_left(x).start()
        return carry

    lax.fori_loop(0, planes, hamiltonian, 0)

    def relay_right(x):
        return remote(phi.at[x, left], phi.at[x, left], relay_send.at[x], relay_recv.at[x], "band", right)

    def relay_left(x):
        return remote(phi.at[x, right], phi.at[x, right], relay_send.at[x], relay_recv.at[x], "band", left)

    product[...] = jnp.zeros_like(product)
    pairs = planes // 2

    def gather(i, carry):
        @pl.when(i < pairs)
        def _():
            for slot, relay in ((0, relay_right), (1, relay_left)):
                x = 2 * i + slot
                stage(x, slot).wait()
                stacked[x] = halves(staged[slot])

                @pl.when(i < pairs - 1)
                def _(x=x, slot=slot):
                    stage(x + 2, slot).start()

                to_right(x).wait_recv()
                to_left(x).wait_recv()
                relay(x).start()

        @pl.when(i > 0)
        def _():
            for slot, relay in ((0, relay_right), (1, relay_left)):
                x = 2 * i - 2 + slot
                relay(x).wait_recv()
                relay(x).wait_send()
                to_right(x).wait_send()
                to_left(x).wait_send()
                product[...] += dot_nt(halves(phi[x].reshape(count, cells)), stacked[x])

        return carry

    lax.fori_loop(0, pairs + 1, gather, 0)

    folded = product[pl.ds(0, count), :] + product[pl.ds(count, count), :]
    folded = folded + pltpu.roll(folded, 64, axis=1)
    correlation = all_reduce(folded, ((0, "gx", gx, nx), (1, "gy", gy, ny)), slots, sum_send, sum_recv)
    weights = halves(correlation * (1.0 / ncells))

    def removed(x, store):
        for start in range(0, cells, WIDE):
            both = dot(weights, stacked[x, :, pl.ds(start, WIDE)])
            store(start, both[:count] + both[count:])

    half = count // 2

    def across_copies(p):
        return (
            remote(opposite.at[p, pl.ds(0, half)], opposite_in.at[0, p], opp_send.at[0, p], opp_recv.at[0, p], "band", right),
            remote(opposite.at[p, pl.ds(half, half)], opposite_in.at[1, p], opp_send.at[1, p], opp_recv.at[1, p], "band", left),
        )

    def side_copy(side, p):
        return remote(sides.at[side, p], sides_in.at[side, p], side_send.at[side, p], side_recv.at[side, p], "band", (right, left)[side])

    def send_across(p, carry):
        def store(start, value):
            opposite[p, :, pl.ds(start, WIDE)] = value

        removed(across * quarter + p, store)
        for copy in across_copies(p):
            copy.start()
        return carry

    lax.fori_loop(0, quarter, send_across, 0)

    def send_sides(p, carry):
        for side in range(2):

            def store(start, value, side=side):
                sides[side, p, :, pl.ds(start, WIDE)] = value

            removed((right, left)[side] * quarter + p, store)
        for side in range(2):
            copy = across_copies(p)[side]
            copy.wait_recv()
            copy.wait_send()
            sides[side, p, pl.ds(side * half, half)] += opposite_in[side, p]
            side_copy(side, p).start()
        return carry

    lax.fori_loop(0, quarter, send_sides, 0)

    def own_part(p, carry):
        x = band * quarter + p

        def store(start, value):
            projected[p, :, pl.ds(start, WIDE)] = phi[x, :, :, pl.ds(start, WIDE)].reshape(count, WIDE) - value

        removed(x, store)
        return carry

    lax.fori_loop(0, quarter, own_part, 0)

    product[...] = jnp.zeros_like(product)

    def inner_products(p, carry):
        for side in range(2):
            side_copy(side, p).wait_recv()
            side_copy(side, p).wait_send()
        for start in range(0, cells, WIDE):
            at = pl.ds(start, WIDE)
            pieces[p, :, at] = halves(projected[p, :, at] - (sides_in[0, p, :, at] + sides_in[1, p, :, at]))
        both = pieces[p]
        product[...] += dot_nt(both, jnp.concatenate([both, both], axis=0))
        return carry

    lax.fori_loop(0, quarter, inner_products, 0)

    folded = product[pl.ds(0, count), :] + product[pl.ds(count, count), :]
    folded = folded + pltpu.roll(folded, count, axis=1)
    gram = all_reduce(
        folded, ((2, "gx", gx, nx), (3, "gy", gy, ny), (4, "band", band, nb)), slots, sum_send, sum_recv
    )
    inverse = halves(inverse_factor(gram * (1.0 / ncells)))[:, : 2 * count]

    def back(p, k):
        return remote(
            result.at[p, lax.rem(band + k, nb)], out.at[band * quarter + p],
            back_send.at[p, k - 1], back_recv.at[p, k - 1], "band", lax.rem(band + k, nb),
        )

    def keep(p):
        return pltpu.make_async_copy(result.at[p, band], out.at[band * quarter + p], local_sem.at[p])

    def finish(p, carry):
        for start in range(0, cells, WIDE):
            at = pl.ds(start, WIDE)
            both = dot(inverse, pieces[p, :, at])
            result[p, :, :, at] = (both[:count] + both[count:]).reshape(nb, own, WIDE)
        for k in (2, 1, 3):
            back(p, k).start()
        keep(p).start()
        return carry

    lax.fori_loop(0, quarter, finish, 0)

    def drain(p, carry):
        for k in range(1, nb):
            back(p, k).wait()
        keep(p).wait()
        return carry

    lax.fori_loop(0, quarter, drain, 0)


def shards(sizes, block, prior, potential):
    nx, ny, nb = sizes
    block_x, prior_x = block.transpose(1, 0, 2), prior.transpose(1, 0, 2)
    planes, own, cells = block_x.shape
    priors, count, quarter = prior_x.shape[1], own * nb, planes // nb
    ncells = planes * nx * cells * ny
    dma = pltpu.SemaphoreType.DMA
    most = max(sizes)
    out = pl.pallas_call(
        functools.partial(kernel, sizes, ncells),
        out_shape=jax.ShapeDtypeStruct(block_x.shape, F32),
        in_specs=[
            pl.BlockSpec(memory_space=pl.ANY),
            pl.BlockSpec(memory_space=pl.ANY),
            pl.BlockSpec(memory_space=pltpu.VMEM),
        ],
        out_specs=pl.BlockSpec(memory_space=pl.ANY),
        scratch_shapes=[
            pltpu.VMEM((planes + 8, own, cells + 2 * WIDTH), F32),
            pltpu.VMEM((planes, nb, own, cells), F32),
            pltpu.VMEM((2, priors, cells), F32),
            pltpu.VMEM((planes, 2 * priors, cells), BF16),
            pltpu.VMEM((2 * count, 128), F32),
            pltpu.VMEM((quarter, count, cells), F32),
            pltpu.VMEM((2, quarter, count, cells), F32),
            pltpu.VMEM((2, quarter, count // 2, cells), F32),
            pltpu.VMEM((2, quarter, count, cells), F32),
            pltpu.VMEM((quarter, count, cells), F32),
            pltpu.VMEM((quarter, 2 * count, cells), BF16),
            pltpu.VMEM((quarter, nb, own, cells), F32),
            pltpu.VMEM((5, most, count, 128), F32),
            dma((quarter,)),
            dma((2,)),
            dma((4,)),
            dma((4,)),
            dma((2, planes)),
            dma((2, planes)),
            dma((planes,)),
            dma((planes,)),
            dma((2, quarter)),
            dma((2, quarter)),
            dma((2, quarter)),
            dma((2, quarter)),
            dma((5, most)),
            dma((5, most)),
            dma((quarter, nb)),
            dma((quarter, nb)),
        ],
        compiler_params=pltpu.CompilerParams(
            collective_id=0, has_side_effects=True, vmem_limit_bytes=67000000
        ),
    )(block_x, prior_x, potential)
    return out.transpose(1, 0, 2)


def solution(mesh):
    sizes = tuple(mesh.shape[a] for a in ("gx", "gy", "band"))
    in_specs = (P("band", "gx", "gy"), P("band", "gx", "gy"), P("gx", "gy"))
    out_specs = P("band", "gx", "gy")
    return jax.shard_map(
        functools.partial(shards, sizes), mesh=mesh, in_specs=in_specs, out_specs=out_specs, check_vma=False
    )
```

time: 603 us -> 184 us (0.31)
  blocking collectives: 257 us -> 0 us
  waiting for transfers between devices: 229 us -> 0 us
  Pallas kernels: 0 us -> 181 us
  matrix products: 42 us -> 0 us
  other arithmetic: 35.5 us -> 0 us
  local copies, waits for them, and re-layouts: 17.2 us -> 2.8 us
  between operations: 13.3 us -> 0.01 us
  starting transfers between devices: 8.78 us -> 0 us
    psum x2 -> x0, blocking collectives: 257 us -> none  [the longest x1 129 us: shards(): gram = lax.psum(matmul(projected, projected.T), ('gx', 'gy')) / ncells_all]
    pallas_call x0 -> x1, Pallas kernels: none -> 181 us  [shards(): pl.pallas_call(functools.partial(kernel, sizes, ncells), out_shape=jax.Sh...]
    all_gather x2 -> x0, waiting for transfers between devices: 151 us -> none  [the longest x1 79.2 us: shards(): phi_all = lax.all_gather(phi_flat, 'band', axis=0, tiled=True)]
    reduce_scatter x1 -> x0, waiting for transfers between devices: 66.2 us -> none  [shards(): lax.psum_scatter(matmul(correlation.T, prior_flat), 'band', scatter_dimen...]
    dot_general x4 -> x0, matrix products: 41.8 us -> none  [matmul(): jnp.dot(left, right, precision=lax.Precision.HIGHEST, preferred_element_t...]
    mul x1 -> x0, other arithmetic: 20.7 us -> none  [shards(): phi = -2.0 * lap_flat + potential[None] * block]
    reshape x2 -> x0, local copies, waits for them, and re-layouts: 13.3 us -> none  [the longest x1 11.4 us: shards(): prior_flat = prior.reshape(prior.shape[0], -1)]
    ppermute x4 -> x0, waiting for transfers between devices: 11.7 us -> none  [the longest x2 9.66 us: extended_2(): after = lax.ppermute(leading, axis, down)]
  transfers between devices with their start and end apart: 7 -> 0, of which waited for: 7 -> 0; matrix products, arithmetic and copies ran while one was open for 2% -> 0% of each run, Pallas kernels for 0% -> 0%
where the time goes in v1:
time: 184 us
  Pallas kernels  181 us (98%)
  local copies, waits for them, and re-layouts  2.8 us (2%)
    pallas_call x1, Pallas kernels, shards(): pl.pallas_call(functools.partial(kernel, sizes, ncells), out_shape=jax.Sh...  181 us

profile of v1, /device:TPU:0, one launch (start us, length us, event | category | flops | bytes accessed | tf_op | source)
XLA Modules:
  0.0 184.1 jit_solution(16316625220707208935)
XLA Ops:
  0.0 181.3 %shard_map.37 = f32[12,8,4608]{2,1,0:T(8,128)} custom-call(f32[12,8,4608]{2,1,0:T(8,128)} %bitcast.5, f32[12,64,4608]{2,1,0:T(8,128)} %bitcast.3, f32[12,4608]{1,0:T(8,128)} %potential.1), custom_call_target="tpu_custom_call" | custom-call | tf_op jit(solution)/shard_map/pallas_call | solution.py:333
  181.3 2.8 %copy.5 = f32[8,12,4608]{2,0,1:T(8,128)} copy(f32[8,12,4608]{2,0,1:T(8,128)} %bitcast.4) | data formatting | bytes 3538944

commit v2 on v1

--- a/solution.py
+++ b/solution.py
@@ -39,21 +39,37 @@
 
 
 def all_reduce(value, stages, slots, send, recv):
+    rows = pl.ds(0, value.shape[0])
     for at, axis, me, n in stages:
-        slots[at, me] = value
+        slots[at, me, rows] = value
         copies = []
         for k in range(1, n):
             copy = remote(
-                slots.at[at, me], slots.at[at, me], send.at[at, k - 1], recv.at[at, k - 1], axis, lax.rem(me + k, n)
+                slots.at[at, me, rows], slots.at[at, me, rows], send.at[at, k - 1], recv.at[at, k - 1], axis, lax.rem(me + k, n)
             )
             copy.start()
             copies.append(copy)
         for copy in copies:
             copy.wait()
-        value = slots[at, 0]
+        value = slots[at, 0, rows]
         for k in range(1, n):
-            value = value + slots[at, k]
+            value = value + slots[at, k, rows]
     return value
+
+
+def pack(value, parts):
+    rows, lanes = value.shape[0] // parts, value.shape[1] // parts
+    group = lax.broadcasted_iota(jnp.int32, (rows, value.shape[1]), 1) // lanes
+    packed = value[:rows]
+    for k in range(1, parts):
+        packed = jnp.where(group == k, value[k * rows : (k + 1) * rows], packed)
+    return packed
+
+
+def unpack(packed, parts):
+    width = packed.shape[1]
+    moved = [packed] + [pltpu.roll(packed, width - k * (width // parts), axis=1) for k in range(1, parts)]
+    return jnp.concatenate(moved, axis=0)
 
 
 def inverse_factor(gram):
@@ -72,9 +88,10 @@
 
 def kernel(
     sizes, ncells, block, prior, potential, out,
-    grid, phi, staged, stacked, product, opposite, sides, opposite_in, sides_in, projected, pieces, result, slots,
+    grid, phi, staged, stacked, product, opposite, sides, opposite_in, sides_in, projected, pieces, result, passing, slots,
     local_sem, stage_sem, halo_send, halo_recv, ring_send, ring_recv, relay_send, relay_recv,
     opp_send, opp_recv, side_send, side_recv, sum_send, sum_recv, back_send, back_recv,
+    hop_send, hop_recv, last_send, last_recv,
 ):
     nx, ny, nb = sizes
     gx, gy, band = lax.axis_index("gx"), lax.axis_index("gy"), lax.axis_index("band")
@@ -89,8 +106,8 @@
     def stage(x, slot):
         return pltpu.make_async_copy(prior.at[x], staged.at[slot], stage_sem.at[slot])
 
-    stage(0, 0).start()
-    stage(1, 1).start()
+    stage(4, 0).start()
+    stage(5, 1).start()
 
     barrier = pltpu.get_barrier_semaphore()
     for axis, me, n in (("gx", gx, nx), ("gy", gy, ny), ("band", band, nb)):
@@ -99,12 +116,22 @@
     pl.semaphore_wait(barrier, nx + ny + nb - 3)
 
     middle = pl.ds(WIDTH, cells)
-    inner = pl.ds(4, planes)
+    low, high = pl.ds(0, WIDTH), pl.ds(cells - WIDTH, WIDTH)
+    above = pl.ds(WIDTH + cells, WIDTH)
+
+    def y_halos(at, first, size):
+        here, there = pl.ds(first, size), pl.ds(4 + first, size)
+        return (
+            (at, "gy", gy, ny, 1, block.at[here, :, high], grid.at[there, :, low]),
+            (at + 1, "gy", gy, ny, -1, block.at[here, :, low], grid.at[there, :, above]),
+        )
+
     halos = (
-        (0, "gx", gx, nx, 1, block.at[pl.ds(planes - 4, 4)], grid.at[pl.ds(0, 4), :, middle]),
-        (1, "gx", gx, nx, -1, block.at[pl.ds(0, 4)], grid.at[pl.ds(planes + 4, 4), :, middle]),
-        (2, "gy", gy, ny, 1, block.at[:, :, pl.ds(cells - WIDTH, WIDTH)], grid.at[inner, :, pl.ds(0, WIDTH)]),
-        (3, "gy", gy, ny, -1, block.at[:, :, pl.ds(0, WIDTH)], grid.at[inner, :, pl.ds(WIDTH + cells, WIDTH)]),
+        *y_halos(0, 4, planes - 8),
+        (2, "gx", gx, nx, 1, block.at[pl.ds(planes - 4, 4)], grid.at[pl.ds(0, 4), :, middle]),
+        (3, "gx", gx, nx, -1, block.at[pl.ds(0, 4)], grid.at[pl.ds(planes + 4, 4), :, middle]),
+        *y_halos(4, planes - 4, 4),
+        *y_halos(6, 0, 4),
     )
 
     def halo(at, axis, me, n, step, src, dst):
@@ -124,10 +151,12 @@
             dst[...] = jnp.zeros(dst.shape, F32)
 
     fill.wait()
-    for entry in halos:
-        copy, sends, receives, dst = halo(*entry)
-        pl.when(receives)(copy.wait_recv)
-        pl.when(sends)(copy.wait_send)
+
+    def arrive(entries):
+        for entry in entries:
+            copy, sends, receives, dst = halo(*entry)
+            pl.when(receives)(copy.wait_recv)
+            pl.when(sends)(copy.wait_send)
 
     depth = lax.rem(lax.broadcasted_iota(jnp.int32, (own, CHUNK), 1), NZ)
     ups = [jnp.where(depth < NZ - m, coeffs[m], 0.0).astype(F32) for m in range(1, 5)]
@@ -139,7 +168,11 @@
     def to_left(x):
         return remote(phi.at[x, band], phi.at[x, band], ring_send.at[1, x], ring_recv.at[1, x], "band", left)
 
-    def hamiltonian(x, carry):
+    def place(i):
+        return lax.rem(i + 4, planes)
+
+    def hamiltonian(i, carry):
+        x = place(i)
         for start in range(0, cells, CHUNK):
             s = WIDTH + start
             center = grid[x + 4, :, pl.ds(s, CHUNK)]
@@ -169,7 +202,10 @@
         to_left(x).start()
         return carry
 
-    lax.fori_loop(0, planes, hamiltonian, 0)
+    arrive(halos[:2])
+    lax.fori_loop(0, planes - 8, hamiltonian, 0)
+    arrive(halos[2:])
+    lax.fori_loop(planes - 8, planes, hamiltonian, 0)
 
     def relay_right(x):
         return remote(phi.at[x, left], phi.at[x, left], relay_send.at[x], relay_recv.at[x], "band", right)
@@ -184,13 +220,13 @@
         @pl.when(i < pairs)
         def _():
             for slot, relay in ((0, relay_right), (1, relay_left)):
-                x = 2 * i + slot
+                x = place(2 * i + slot)
                 stage(x, slot).wait()
                 stacked[x] = halves(staged[slot])
 
                 @pl.when(i < pairs - 1)
                 def _(x=x, slot=slot):
-                    stage(x + 2, slot).start()
+                    stage(lax.rem(x + 2, planes), slot).start()
 
                 to_right(x).wait_recv()
                 to_left(x).wait_recv()
@@ -199,7 +235,7 @@
         @pl.when(i > 0)
         def _():
             for slot, relay in ((0, relay_right), (1, relay_left)):
-                x = 2 * i - 2 + slot
+                x = place(2 * i - 2 + slot)
                 relay(x).wait_recv()
                 relay(x).wait_send()
                 to_right(x).wait_send()
@@ -212,8 +248,11 @@
 
     folded = product[pl.ds(0, count), :] + product[pl.ds(count, count), :]
     folded = folded + pltpu.roll(folded, 64, axis=1)
-    correlation = all_reduce(folded, ((0, "gx", gx, nx), (1, "gy", gy, ny)), slots, sum_send, sum_recv)
-    weights = halves(correlation * (1.0 / ncells))
+    packed = all_reduce(pack(folded, 2), ((0, "gx", gx, nx), (1, "gy", gy, ny)), slots, sum_send, sum_recv)
+    correlation = unpack(packed, 2) * (1.0 / ncells)
+    lane = lax.broadcasted_iota(jnp.int32, correlation.shape, 1)
+    correlation = jnp.where(lane < 64, correlation, pltpu.roll(correlation, 64, axis=1))
+    weights = halves(correlation)
 
     def removed(x, store):
         for start in range(0, cells, WIDE):
@@ -287,15 +326,31 @@
 
     folded = product[pl.ds(0, count), :] + product[pl.ds(count, count), :]
     folded = folded + pltpu.roll(folded, count, axis=1)
-    gram = all_reduce(
-        folded, ((2, "gx", gx, nx), (3, "gy", gy, ny), (4, "band", band, nb)), slots, sum_send, sum_recv
+    packed = all_reduce(
+        pack(folded, 4), ((2, "gx", gx, nx), (3, "gy", gy, ny), (4, "band", band, nb)), slots, sum_send, sum_recv
     )
-    inverse = halves(inverse_factor(gram * (1.0 / ncells)))[:, : 2 * count]
-
-    def back(p, k):
+    inverse = halves(inverse_factor(unpack(packed, 4) * (1.0 / ncells)))[:, : 2 * count]
+
+    split = cells // 2
+
+    def back(p, side):
+        peer = (right, left)[side]
         return remote(
-            result.at[p, lax.rem(band + k, nb)], out.at[band * quarter + p],
-            back_send.at[p, k - 1], back_recv.at[p, k - 1], "band", lax.rem(band + k, nb),
+            result.at[p, peer], out.at[band * quarter + p], back_send.at[side, p], back_recv.at[side, p], "band", peer
+        )
+
+    def first_hop(p, side):
+        part = pl.ds(side * split, split)
+        return remote(
+            result.at[p, across, :, part], passing.at[side, p],
+            hop_send.at[side, p], hop_recv.at[side, p], "band", (right, left)[side],
+        )
+
+    def second_hop(p, side):
+        part = pl.ds(side * split, split)
+        return remote(
+            passing.at[side, p], out.at[(left, right)[side] * quarter + p, :, part],
+            last_send.at[side, p], last_recv.at[side, p], "band", (right, left)[side],
         )
 
     def keep(p):
@@ -306,16 +361,27 @@
             at = pl.ds(start, WIDE)
             both = dot(inverse, pieces[p, :, at])
             result[p, :, :, at] = (both[:count] + both[count:]).reshape(nb, own, WIDE)
-        for k in (2, 1, 3):
-            back(p, k).start()
+        for side in range(2):
+            first_hop(p, side).start()
+        for side in range(2):
+            back(p, side).start()
         keep(p).start()
         return carry
 
     lax.fori_loop(0, quarter, finish, 0)
 
+    def forward(p, carry):
+        for side in range(2):
+            first_hop(p, side).wait()
+            second_hop(p, side).start()
+        return carry
+
+    lax.fori_loop(0, quarter, forward, 0)
+
     def drain(p, carry):
-        for k in range(1, nb):
-            back(p, k).wait()
+        for side in range(2):
+            back(p, side).wait()
+            second_hop(p, side).wait()
         keep(p).wait()
         return carry
 
@@ -352,11 +418,12 @@
             pltpu.VMEM((quarter, count, cells), F32),
             pltpu.VMEM((quarter, 2 * count, cells), BF16),
             pltpu.VMEM((quarter, nb, own, cells), F32),
-            pltpu.VMEM((5, most, count, 128), F32),
+            pltpu.VMEM((2, quarter, own, cells // 2), F32),
+            pltpu.VMEM((5, most, count // 2, 128), F32),
             dma((quarter,)),
             dma((2,)),
-            dma((4,)),
-            dma((4,)),
+            dma((8,)),
+            dma((8,)),
             dma((2, planes)),
             dma((2, planes)),
             dma((planes,)),
@@ -367,8 +434,7 @@
             dma((2, quarter)),
             dma((5, most)),
             dma((5, most)),
-            dma((quarter, nb)),
-            dma((quarter, nb)),
+            *[dma((2, quarter))] * 6,
         ],
         compiler_params=pltpu.CompilerParams(
             collective_id=0, has_side_effects=True, vmem_limit_bytes=67000000

time: 184 us -> 180 us (0.978)
  Pallas kernels: 181 us -> 177 us
    pallas_call x1, Pallas kernels: 181 us -> 177 us  [shards(): pl.pallas_call(functools.partial(kernel, sizes, ncells), out_shape=jax.Sh...]
where the time goes in v2:
time: 180 us
  Pallas kernels  177 us (98%)
  local copies, waits for them, and re-layouts  2.8 us (2%)
    pallas_call x1, Pallas kernels, shards(): pl.pallas_call(functools.partial(kernel, sizes, ncells), out_shape=jax.Sh...  177 us

profile of v2, /device:TPU:0, one launch (start us, length us, event | category | flops | bytes accessed | tf_op | source)
XLA Modules:
  0.0 179.9 jit_solution(3337545890456092905)
XLA Ops:
  0.0 177.1 %shard_map.37 = f32[12,8,4608]{2,1,0:T(8,128)} custom-call(f32[12,8,4608]{2,1,0:T(8,128)} %bitcast.5, f32[12,64,4608]{2,1,0:T(8,128)} %bitcast.3, f32[12,4608]{1,0:T(8,128)} %potential.1), custom_call_target="tpu_custom_call" | custom-call | tf_op jit(solution)/shard_map/pallas_call | solution.py:399
  177.1 2.8 %copy.5 = f32[8,12,4608]{2,0,1:T(8,128)} copy(f32[8,12,4608]{2,0,1:T(8,128)} %bitcast.4) | data formatting | bytes 3538944

commit v3 on v2

--- a/solution.py
+++ b/solution.py
@@ -38,23 +38,9 @@
     )
 
 
-def all_reduce(value, stages, slots, send, recv):
-    rows = pl.ds(0, value.shape[0])
-    for at, axis, me, n in stages:
-        slots[at, me, rows] = value
-        copies = []
-        for k in range(1, n):
-            copy = remote(
-                slots.at[at, me, rows], slots.at[at, me, rows], send.at[at, k - 1], recv.at[at, k - 1], axis, lax.rem(me + k, n)
-            )
-            copy.start()
-            copies.append(copy)
-        for copy in copies:
-            copy.wait()
-        value = slots[at, 0, rows]
-        for k in range(1, n):
-            value = value + slots[at, k, rows]
-    return value
+def stacked_halves(value):
+    high = value.astype(BF16).astype(F32)
+    return jnp.concatenate([high, value - high], axis=0).astype(BF16)
 
 
 def pack(value, parts):
@@ -139,10 +125,12 @@
         sends, receives = (me < n - 1, me > 0) if step == 1 else (me > 0, me < n - 1)
         return copy, sends, receives, dst
 
-    for entry in halos:
-        copy, sends, receives, dst = halo(*entry)
-        pl.when(sends)(copy.start)
-
+    def depart(entries):
+        for entry in entries:
+            copy, sends, receives, dst = halo(*entry)
+            pl.when(sends)(copy.start)
+
+    depart(halos[:4])
     for entry in halos:
         copy, sends, receives, dst = halo(*entry)
 
@@ -163,10 +151,10 @@
     downs = [jnp.where(depth >= m, coeffs[m], 0.0).astype(F32) for m in range(1, 5)]
 
     def to_right(x):
-        return remote(phi.at[x, band], phi.at[x, band], ring_send.at[0, x], ring_recv.at[0, x], "band", right)
+        return remote(phi.at[x, 0], phi.at[x, 1], ring_send.at[0, x], ring_recv.at[0, x], "band", right)
 
     def to_left(x):
-        return remote(phi.at[x, band], phi.at[x, band], ring_send.at[1, x], ring_recv.at[1, x], "band", left)
+        return remote(phi.at[x, 0], phi.at[x, 2], ring_send.at[1, x], ring_recv.at[1, x], "band", left)
 
     def place(i):
         return lax.rem(i + 4, planes)
@@ -197,139 +185,225 @@
                 total = total + ups[m - 1] * pltpu.roll(center, CHUNK - m, axis=1)
                 total = total + downs[m - 1] * pltpu.roll(center, m, axis=1)
             weight = potential[pl.ds(x, 1), pl.ds(start, CHUNK)]
-            phi[x, band, :, pl.ds(start, CHUNK)] = weight * center - 2.0 * total
+            phi[x, 0, :, pl.ds(start, CHUNK)] = weight * center - 2.0 * total
         to_right(x).start()
         to_left(x).start()
         return carry
 
     arrive(halos[:2])
+    depart(halos[4:])
     lax.fori_loop(0, planes - 8, hamiltonian, 0)
     arrive(halos[2:])
     lax.fori_loop(planes - 8, planes, hamiltonian, 0)
 
     def relay_right(x):
-        return remote(phi.at[x, left], phi.at[x, left], relay_send.at[x], relay_recv.at[x], "band", right)
+        return remote(phi.at[x, 1], phi.at[x, 3], relay_send.at[x], relay_recv.at[x], "band", right)
 
     def relay_left(x):
-        return remote(phi.at[x, right], phi.at[x, right], relay_send.at[x], relay_recv.at[x], "band", left)
-
+        return remote(phi.at[x, 2], phi.at[x, 3], relay_send.at[x], relay_recv.at[x], "band", left)
+
+    relays = (relay_right, relay_left)
     product[...] = jnp.zeros_like(product)
     pairs = planes // 2
-
-    def gather(i, carry):
-        @pl.when(i < pairs)
+    near = 3 * own
+    early_rows, late_rows, gram_rows = pl.ds(0, 2 * near), pl.ds(2 * near, 2 * own), pl.ds(2 * count, 2 * count)
+
+    def gather_near(i, carry):
+        x, slot = place(i), lax.rem(i, 2)
+        stage(x, slot).wait()
+        stacked[x] = halves(staged[slot])
+
+        @pl.when(i < planes - 2)
         def _():
-            for slot, relay in ((0, relay_right), (1, relay_left)):
-                x = place(2 * i + slot)
-                stage(x, slot).wait()
-                stacked[x] = halves(staged[slot])
-
-                @pl.when(i < pairs - 1)
-                def _(x=x, slot=slot):
-                    stage(lax.rem(x + 2, planes), slot).start()
-
-                to_right(x).wait_recv()
-                to_left(x).wait_recv()
-                relay(x).start()
-
-        @pl.when(i > 0)
-        def _():
-            for slot, relay in ((0, relay_right), (1, relay_left)):
-                x = place(2 * i - 2 + slot)
-                relay(x).wait_recv()
-                relay(x).wait_send()
-                to_right(x).wait_send()
-                to_left(x).wait_send()
-                product[...] += dot_nt(halves(phi[x].reshape(count, cells)), stacked[x])
-
-        return carry
-
-    lax.fori_loop(0, pairs + 1, gather, 0)
-
-    folded = product[pl.ds(0, count), :] + product[pl.ds(count, count), :]
+            stage(place(i + 2), slot).start()
+
+        to_right(x).wait_recv()
+        to_left(x).wait_recv()
+        product[early_rows, :] += dot_nt(stacked_halves(phi[x, 0:3].reshape(near, cells)), stacked[x])
+        return carry
+
+    def start_relays(i, carry):
+        for k in range(2):
+            relays[k](place(2 * i + k)).start()
+        return carry
+
+    def gather_far(i, carry):
+        for k in range(2):
+            x = place(2 * i + k)
+            relays[k](x).wait()
+            to_right(x).wait_send()
+            to_left(x).wait_send()
+            product[late_rows, :] += dot_nt(stacked_halves(phi[x, 3]), stacked[x])
+        return carry
+
+    def sum_start(at, axis, me, n, value):
+        rows = pl.ds(0, value.shape[0])
+        slots[at, me, rows] = value
+        for k in range(1, n):
+            sum_copy(at, axis, me, n, rows, k).start()
+
+    def sum_copy(at, axis, me, n, rows, k):
+        return remote(
+            slots.at[at, me, rows], slots.at[at, me, rows],
+            sum_send.at[at, k - 1], sum_recv.at[at, k - 1], axis, lax.rem(me + k, n),
+        )
+
+    def sum_finish(at, axis, me, n, size):
+        rows = pl.ds(0, size)
+        for k in range(1, n):
+            sum_copy(at, axis, me, n, rows, k).wait()
+        value = slots[at, 0, rows]
+        for k in range(1, n):
+            value = value + slots[at, k, rows]
+        return value
+
+    lax.fori_loop(0, planes - 2, gather_near, 0)
+    lax.fori_loop(0, pairs - 1, start_relays, 0)
+    lax.fori_loop(planes - 2, planes, gather_near, 0)
+    start_relays(pairs - 1, 0)
+
+    scale = 1.0 / ncells
+    lane = lax.broadcasted_iota(jnp.int32, (own, 128), 1)
+    folded = product[pl.ds(0, near), :] + product[pl.ds(near, near), :]
     folded = folded + pltpu.roll(folded, 64, axis=1)
-    packed = all_reduce(pack(folded, 2), ((0, "gx", gx, nx), (1, "gy", gy, ny)), slots, sum_send, sum_recv)
-    correlation = unpack(packed, 2) * (1.0 / ncells)
-    lane = lax.broadcasted_iota(jnp.int32, correlation.shape, 1)
-    correlation = jnp.where(lane < 64, correlation, pltpu.roll(correlation, 64, axis=1))
-    weights = halves(correlation)
-
-    def removed(x, store):
+    first = jnp.where(lane < 64, folded[:own], folded[own : 2 * own])
+    sum_start(0, "gx", gx, nx, jnp.concatenate([first, folded[2 * own :]], axis=0))
+    gather_far(0, 0)
+    sum_start(1, "gy", gy, ny, sum_finish(0, "gx", gx, nx, 2 * own))
+    gather_far(1, 0)
+    packed = sum_finish(1, "gy", gy, ny, 2 * own) * scale
+    first, third = packed[:own], packed[own:]
+    other = pltpu.roll(first, 64, axis=1)
+    near_weights = stacked_halves(
+        jnp.concatenate([jnp.where(lane < 64, first, other), jnp.where(lane < 64, other, first), third], axis=0)
+    )
+
+    def removed_near(x, store):
         for start in range(0, cells, WIDE):
-            both = dot(weights, stacked[x, :, pl.ds(start, WIDE)])
-            store(start, both[:count] + both[count:])
-
-    half = count // 2
-
-    def across_copies(p):
-        return (
-            remote(opposite.at[p, pl.ds(0, half)], opposite_in.at[0, p], opp_send.at[0, p], opp_recv.at[0, p], "band", right),
-            remote(opposite.at[p, pl.ds(half, half)], opposite_in.at[1, p], opp_send.at[1, p], opp_recv.at[1, p], "band", left),
-        )
-
-    def side_copy(side, p):
-        return remote(sides.at[side, p], sides_in.at[side, p], side_send.at[side, p], side_recv.at[side, p], "band", (right, left)[side])
+            both = dot(near_weights, stacked[x, :, pl.ds(start, WIDE)])
+            store(pl.ds(start, WIDE), (both[:near] + both[near:]).reshape(3, own, WIDE))
+
+    def across_copy(side, p, j):
+        return remote(
+            opposite.at[p, ((2, 0), (1, 3))[side][j]], opposite_in.at[side, p, j],
+            opp_send.at[side, p, j], opp_recv.at[side, p, j], "band", (right, left)[side],
+        )
+
+    def side_copy(side, p, r):
+        return remote(
+            sides.at[side, p, r], sides_in.at[side, p, ((1, 3, 0, 2), (2, 0, 3, 1))[side][r]],
+            side_send.at[side, p, r], side_recv.at[side, p, ((1, 3, 0, 2), (2, 0, 3, 1))[side][r]],
+            "band", (right, left)[side],
+        )
 
     def send_across(p, carry):
-        def store(start, value):
-            opposite[p, :, pl.ds(start, WIDE)] = value
-
-        removed(across * quarter + p, store)
-        for copy in across_copies(p):
-            copy.start()
+        def store(at, value):
+            opposite[p, 0:3, :, at] = value
+
+        removed_near(across * quarter + p, store)
+        for side, j in ((0, 0), (0, 1), (1, 0)):
+            across_copy(side, p, j).start()
+        return carry
+
+    def send_direct(p, carry):
+        for side in range(2):
+
+            def store(at, value, side=side):
+                sides[side, p, 0:3, :, at] = value
+
+            removed_near((right, left)[side] * quarter + p, store)
+            side_copy(side, p, 2).start()
+        return carry
+
+    def add_and_send(side, p, j):
+        across_copy(side, p, j).wait()
+        sides[side, p, j] += opposite_in[side, p, j]
+        side_copy(side, p, j).start()
+
+    def relay_sums(p, carry):
+        for side, j in ((1, 0), (0, 0), (0, 1)):
+            add_and_send(side, p, j)
         return carry
 
     lax.fori_loop(0, quarter, send_across, 0)
-
-    def send_sides(p, carry):
-        for side in range(2):
-
-            def store(start, value, side=side):
-                sides[side, p, :, pl.ds(start, WIDE)] = value
-
-            removed((right, left)[side] * quarter + p, store)
-        for side in range(2):
-            copy = across_copies(p)[side]
-            copy.wait_recv()
-            copy.wait_send()
-            sides[side, p, pl.ds(side * half, half)] += opposite_in[side, p]
-            side_copy(side, p).start()
-        return carry
-
-    lax.fori_loop(0, quarter, send_sides, 0)
+    lax.fori_loop(0, quarter, send_direct, 0)
+    lax.fori_loop(2, pairs, gather_far, 0)
+    folded = product[pl.ds(2 * near, own), :] + product[pl.ds(2 * near + own, own), :]
+    sum_start(5, "gx", gx, nx, folded + pltpu.roll(folded, 64, axis=1))
+    lax.fori_loop(0, quarter - 1, relay_sums, 0)
+    sum_start(6, "gy", gy, ny, sum_finish(5, "gx", gx, nx, own))
+    lax.fori_loop(quarter - 1, quarter, relay_sums, 0)
+    far_weights = stacked_halves(sum_finish(6, "gy", gy, ny, own) * scale)
+
+    def removed_far(x, store):
+        for start in range(0, cells, WIDE):
+            both = dot(far_weights, stacked[x, :, pl.ds(start, WIDE)])
+            store(pl.ds(start, WIDE), both[:own] + both[own:])
+
+    def send_across_far(p, carry):
+        def store(at, value):
+            opposite[p, 3, :, at] = value
+
+        removed_far(across * quarter + p, store)
+        across_copy(1, p, 1).start()
+        return carry
+
+    def send_direct_far(p, carry):
+        for side in range(2):
+
+            def store(at, value, side=side):
+                sides[side, p, 3, :, at] = value
+
+            removed_far((right, left)[side] * quarter + p, store)
+            side_copy(side, p, 3).start()
+        return carry
+
+    def relay_sums_far(p, carry):
+        add_and_send(1, p, 1)
+        return carry
 
     def own_part(p, carry):
         x = band * quarter + p
 
-        def store(start, value):
-            projected[p, :, pl.ds(start, WIDE)] = phi[x, :, :, pl.ds(start, WIDE)].reshape(count, WIDE) - value
-
-        removed(x, store)
-        return carry
-
+        def store(at, value):
+            projected[p, 0:3, :, at] = phi[x, 0:3, :, at] - value
+
+        def store_far(at, value):
+            projected[p, 3, :, at] = phi[x, 3, :, at] - value
+
+        removed_near(x, store)
+        removed_far(x, store_far)
+        return carry
+
+    lax.fori_loop(0, quarter, send_across_far, 0)
+    lax.fori_loop(0, quarter, send_direct_far, 0)
+    lax.fori_loop(0, quarter, relay_sums_far, 0)
     lax.fori_loop(0, quarter, own_part, 0)
-
-    product[...] = jnp.zeros_like(product)
+    slabs = (band, left, right, across)
 
     def inner_products(p, carry):
         for side in range(2):
-            side_copy(side, p).wait_recv()
-            side_copy(side, p).wait_send()
+            for r in range(4):
+                side_copy(side, p, r).wait_send()
+                side_copy(side, p, r).wait_recv()
+        for r in range(4):
+            result[p, slabs[r]] = projected[p, r] - (sides_in[0, p, r] + sides_in[1, p, r])
         for start in range(0, cells, WIDE):
             at = pl.ds(start, WIDE)
-            pieces[p, :, at] = halves(projected[p, :, at] - (sides_in[0, p, :, at] + sides_in[1, p, :, at]))
+            pieces[p, :, at] = halves(result[p, :, :, at].reshape(count, WIDE))
         both = pieces[p]
-        product[...] += dot_nt(both, jnp.concatenate([both, both], axis=0))
+        product[gram_rows, :] += dot_nt(both, jnp.concatenate([both, both], axis=0))
         return carry
 
     lax.fori_loop(0, quarter, inner_products, 0)
 
-    folded = product[pl.ds(0, count), :] + product[pl.ds(count, count), :]
+    folded = product[pl.ds(2 * count, count), :] + product[pl.ds(3 * count, count), :]
     folded = folded + pltpu.roll(folded, count, axis=1)
-    packed = all_reduce(
-        pack(folded, 4), ((2, "gx", gx, nx), (3, "gy", gy, ny), (4, "band", band, nb)), slots, sum_send, sum_recv
-    )
-    inverse = halves(inverse_factor(unpack(packed, 4) * (1.0 / ncells)))[:, : 2 * count]
+    packed = pack(folded, 4)
+    for entry in ((2, "gx", gx, nx), (3, "gy", gy, ny), (4, "band", band, nb)):
+        sum_start(*entry, packed)
+        packed = sum_finish(*entry, own)
+    inverse = halves(inverse_factor(unpack(packed, 4) * scale))[:, : 2 * count]
 
     split = cells // 2
 
@@ -410,16 +484,16 @@
             pltpu.VMEM((planes, nb, own, cells), F32),
             pltpu.VMEM((2, priors, cells), F32),
             pltpu.VMEM((planes, 2 * priors, cells), BF16),
-            pltpu.VMEM((2 * count, 128), F32),
-            pltpu.VMEM((quarter, count, cells), F32),
-            pltpu.VMEM((2, quarter, count, cells), F32),
-            pltpu.VMEM((2, quarter, count // 2, cells), F32),
-            pltpu.VMEM((2, quarter, count, cells), F32),
-            pltpu.VMEM((quarter, count, cells), F32),
+            pltpu.VMEM((4 * count, 128), F32),
+            pltpu.VMEM((quarter, nb, own, cells), F32),
+            pltpu.VMEM((2, quarter, nb, own, cells), F32),
+            pltpu.VMEM((2, quarter, 2, own, cells), F32),
+            pltpu.VMEM((2, quarter, nb, own, cells), F32),
+            pltpu.VMEM((quarter, nb, own, cells), F32),
             pltpu.VMEM((quarter, 2 * count, cells), BF16),
             pltpu.VMEM((quarter, nb, own, cells), F32),
             pltpu.VMEM((2, quarter, own, cells // 2), F32),
-            pltpu.VMEM((5, most, count // 2, 128), F32),
+            pltpu.VMEM((7, most, 2 * own, 128), F32),
             dma((quarter,)),
             dma((2,)),
             dma((8,)),
@@ -428,12 +502,12 @@
             dma((2, planes)),
             dma((planes,)),
             dma((planes,)),
-            dma((2, quarter)),
-            dma((2, quarter)),
-            dma((2, quarter)),
-            dma((2, quarter)),
-            dma((5, most)),
-            dma((5, most)),
+            dma((2, quarter, 2)),
+            dma((2, quarter, 2)),
+            dma((2, quarter, nb)),
+            dma((2, quarter, nb)),
+            dma((7, most)),
+            dma((7, most)),
             *[dma((2, quarter))] * 6,
         ],
         compiler_params=pltpu.CompilerParams(

time: 180 us -> 168 us (0.933)
  Pallas kernels: 177 us -> 165 us
    pallas_call x1, Pallas kernels: 177 us -> 165 us  [shards(): pl.pallas_call(functools.partial(kernel, sizes, ncells), out_shape=jax.Sh...]
where the time goes in v3:
time: 168 us; the launch traced here: 167 us
  Pallas kernels  165 us (98%)
  local copies, waits for them, and re-layouts  2.8 us (2%)
    pallas_call x1, Pallas kernels, shards(): pl.pallas_call(functools.partial(kernel, sizes, ncells), out_shape=jax.Sh...  165 us

profile of v3, /device:TPU:0, one launch (start us, length us, event | category | flops | bytes accessed | tf_op | source)
XLA Modules:
  0.0 167.5 jit_solution(7819064812970204404)
XLA Ops:
  0.0 164.7 %shard_map.37 = f32[12,8,4608]{2,1,0:T(8,128)} custom-call(f32[12,8,4608]{2,1,0:T(8,128)} %bitcast.5, f32[12,64,4608]{2,1,0:T(8,128)} %bitcast.3, f32[12,4608]{1,0:T(8,128)} %potential.1), custom_call_target="tpu_custom_call" | custom-call | tf_op jit(solution)/shard_map/pallas_call | solution.py:473
  164.7 2.8 %copy.5 = f32[8,12,4608]{2,0,1:T(8,128)} copy(f32[8,12,4608]{2,0,1:T(8,128)} %bitcast.4) | data formatting | bytes 3538944

commit v4 on v3

--- a/solution.py
+++ b/solution.py
@@ -73,8 +73,8 @@
 
 
 def kernel(
-    sizes, ncells, block, prior, potential, out,
-    grid, phi, staged, stacked, product, opposite, sides, opposite_in, sides_in, projected, pieces, result, passing, slots,
+    sizes, ncells, block, prior, weights, out,
+    potential, grid, phi, staged, stacked, product, opposite, sides, opposite_in, sides_in, projected, pieces, result, passing, slots,
     local_sem, stage_sem, halo_send, halo_recv, ring_send, ring_recv, relay_send, relay_recv,
     opp_send, opp_recv, side_send, side_recv, sum_send, sum_recv, back_send, back_recv,
     hop_send, hop_recv, last_send, last_recv,
@@ -86,20 +86,21 @@
     count = nb * own
     right, left, across = lax.rem(band + 1, nb), lax.rem(band + nb - 1, nb), lax.rem(band + 2, nb)
 
-    fill = pltpu.make_async_copy(block, grid.at[pl.ds(4, planes), :, pl.ds(WIDTH, cells)], local_sem.at[0])
-    fill.start()
-
-    def stage(x, slot):
-        return pltpu.make_async_copy(prior.at[x], staged.at[slot], stage_sem.at[slot])
-
-    stage(4, 0).start()
-    stage(5, 1).start()
-
     barrier = pltpu.get_barrier_semaphore()
     for axis, me, n in (("gx", gx, nx), ("gy", gy, ny), ("band", band, nb)):
         for k in range(1, n):
             pl.semaphore_signal(barrier, inc=1, device_id={axis: lax.rem(me + k, n)}, device_id_type=MESH)
-    pl.semaphore_wait(barrier, nx + ny + nb - 3)
+
+    fill = pltpu.make_async_copy(block, grid.at[pl.ds(4, planes), :, pl.ds(WIDTH, cells)], local_sem.at[0])
+    fill.start()
+    fill_weights = pltpu.make_async_copy(weights, potential, local_sem.at[1])
+    fill_weights.start()
+
+    def stage(x, slot):
+        return pltpu.make_async_copy(prior.at[x], staged.at[slot], stage_sem.at[slot])
+
+    stage(4, 0).start()
+    stage(5, 1).start()
 
     middle = pl.ds(WIDTH, cells)
     low, high = pl.ds(0, WIDTH), pl.ds(cells - WIDTH, WIDTH)
@@ -130,15 +131,12 @@
             copy, sends, receives, dst = halo(*entry)
             pl.when(sends)(copy.start)
 
-    depart(halos[:4])
     for entry in halos:
         copy, sends, receives, dst = halo(*entry)
 
         @pl.when(jnp.logical_not(receives))
         def _(dst=dst):
             dst[...] = jnp.zeros(dst.shape, F32)
-
-    fill.wait()
 
     def arrive(entries):
         for entry in entries:
@@ -159,9 +157,8 @@
     def place(i):
         return lax.rem(i + 4, planes)
 
-    def hamiltonian(i, carry):
-        x = place(i)
-        for start in range(0, cells, CHUNK):
+    def hamiltonian(x, starts):
+        for start in starts:
             s = WIDTH + start
             center = grid[x + 4, :, pl.ds(s, CHUNK)]
             total = 3.0 * coeffs[0] * center
@@ -186,15 +183,49 @@
                 total = total + downs[m - 1] * pltpu.roll(center, m, axis=1)
             weight = potential[pl.ds(x, 1), pl.ds(start, CHUNK)]
             phi[x, 0, :, pl.ds(start, CHUNK)] = weight * center - 2.0 * total
+
+    def send_part(x, first, size):
+        part = pl.ds(first, size)
+        for side in range(2):
+            remote(
+                phi.at[x, 0, :, part], phi.at[x, 1 + side, :, part],
+                ring_send.at[side, x], ring_recv.at[side, x], "band", (right, left)[side],
+            ).start()
+
+    def inside(i, carry):
+        hamiltonian(place(i), range(WIDTH, cells - WIDTH, CHUNK))
+        return carry
+
+    def send_inside(i, carry):
+        send_part(place(i), WIDTH, cells - 2 * WIDTH)
+        return carry
+
+    def edges(i, carry):
+        x = place(i)
+        for first in (0, cells - WIDTH):
+            hamiltonian(x, range(first, first + WIDTH, CHUNK))
+        for first in (0, cells - WIDTH):
+            send_part(x, first, WIDTH)
+        return carry
+
+    def whole(i, carry):
+        x = place(i)
+        hamiltonian(x, range(0, cells, CHUNK))
         to_right(x).start()
         to_left(x).start()
         return carry
 
+    fill.wait()
+    fill_weights.wait()
+    lax.fori_loop(0, planes - 8, inside, 0)
+    pl.semaphore_wait(barrier, nx + ny + nb - 3)
+    depart(halos[:4])
+    lax.fori_loop(0, planes - 8, send_inside, 0)
     arrive(halos[:2])
     depart(halos[4:])
-    lax.fori_loop(0, planes - 8, hamiltonian, 0)
+    lax.fori_loop(0, planes - 8, edges, 0)
     arrive(halos[2:])
-    lax.fori_loop(planes - 8, planes, hamiltonian, 0)
+    lax.fori_loop(planes - 8, planes, whole, 0)
 
     def relay_right(x):
         return remote(phi.at[x, 1], phi.at[x, 3], relay_send.at[x], relay_recv.at[x], "band", right)
@@ -474,12 +505,13 @@
         functools.partial(kernel, sizes, ncells),
         out_shape=jax.ShapeDtypeStruct(block_x.shape, F32),
         in_specs=[
-            pl.BlockSpec(memory_space=pl.ANY),
-            pl.BlockSpec(memory_space=pl.ANY),
-            pl.BlockSpec(memory_space=pltpu.VMEM),
+            pl.BlockSpec(memory_space=pltpu.HBM),
+            pl.BlockSpec(memory_space=pltpu.HBM),
+            pl.BlockSpec(memory_space=pltpu.HBM),
         ],
         out_specs=pl.BlockSpec(memory_space=pl.ANY),
         scratch_shapes=[
+            pltpu.VMEM((planes, cells), F32),
             pltpu.VMEM((planes + 8, own, cells + 2 * WIDTH), F32),
             pltpu.VMEM((planes, nb, own, cells), F32),
             pltpu.VMEM((2, priors, cells), F32),
@@ -511,7 +543,7 @@
             *[dma((2, quarter))] * 6,
         ],
         compiler_params=pltpu.CompilerParams(
-            collective_id=0, has_side_effects=True, vmem_limit_bytes=67000000
+            collective_id=0, has_side_effects=True, vmem_limit_bytes=53000000
         ),
     )(block_x, prior_x, potential)
     return out.transpose(1, 0, 2)

time: 168 us -> 163 us (0.970)
  Pallas kernels: 165 us -> 160 us
    pallas_call x1, Pallas kernels: 165 us -> 160 us  [shards(): pl.pallas_call(functools.partial(kernel, sizes, ncells), out_shape=jax.Sh...]
where the time goes in v4:
time: 163 us; the launch traced here: 162 us
  Pallas kernels  160 us (98%)
  local copies, waits for them, and re-layouts  2.17 us (1%)
    pallas_call x1, Pallas kernels, shards(): pl.pallas_call(functools.partial(kernel, sizes, ncells), out_shape=jax.Sh...  160 us

profile of v4, /device:TPU:0, one launch (start us, length us, event | category | flops | bytes accessed | tf_op | source)
XLA Modules:
  0.0 162.4 jit_solution(17486974251887915407)
XLA Ops:
  0.0 0.0 copy-start
  0.0 1.0 copy-done
  1.0 160.2 %shard_map.37 = f32[12,8,4608]{2,1,0:T(8,128)S(1)} custom-call(f32[12,8,4608]{2,1,0:T(8,128)} %bitcast.5, f32[12,64,4608]{2,1,0:T(8,128)} %bitcast.4, f32[12,4608]{1,0:T(8,128)S(1)} %copy-done), custom_call_target="tpu_custom_call" | custom-call | tf_op jit(solution)/shard_map/pallas_call | solution.py:504
  161.2 1.2 copy.5
Async XLA Ops:
  0.0 1.0 copy-start

commit v5 on v4

--- a/solution.py
+++ b/solution.py
@@ -423,13 +423,16 @@
             at = pl.ds(start, WIDE)
             pieces[p, :, at] = halves(result[p, :, :, at].reshape(count, WIDE))
         both = pieces[p]
-        product[gram_rows, :] += dot_nt(both, jnp.concatenate([both, both], axis=0))
+        product[gram_rows, pl.ds(0, 2 * count)] += dot_nt(both, both)
         return carry
 
     lax.fori_loop(0, quarter, inner_products, 0)
 
     folded = product[pl.ds(2 * count, count), :] + product[pl.ds(3 * count, count), :]
+    folded = folded + pltpu.roll(folded, 128 - count, axis=1)
+    folded = jnp.where(lax.broadcasted_iota(jnp.int32, folded.shape, 1) < count, folded, 0.0)
     folded = folded + pltpu.roll(folded, count, axis=1)
+    folded = folded + pltpu.roll(folded, 2 * count, axis=1)
     packed = pack(folded, 4)
     for entry in ((2, "gx", gx, nx), (3, "gy", gy, ny), (4, "band", band, nb)):
         sum_start(*entry, packed)

time: 163 us -> 162 us (level)
  no operation moved by 1% of the time
where the time goes in v5:
time: 162 us
  Pallas kernels  160 us (99%)
  local copies, waits for them, and re-layouts  2.17 us (1%)
    pallas_call x1, Pallas kernels, shards(): pl.pallas_call(functools.partial(kernel, sizes, ncells), out_shape=jax.Sh...  160 us

profile of v5, /device:TPU:0, one launch (start us, length us, event | category | flops | bytes accessed | tf_op | source)
XLA Modules:
  0.0 162.3 jit_solution(17729022218347245909)
XLA Ops:
  0.0 0.0 copy-start
  0.0 1.0 copy-done
  1.0 160.1 %shard_map.37 = f32[12,8,4608]{2,1,0:T(8,128)S(1)} custom-call(f32[12,8,4608]{2,1,0:T(8,128)} %bitcast.5, f32[12,64,4608]{2,1,0:T(8,128)} %bitcast.4, f32[12,4608]{1,0:T(8,128)S(1)} %copy-done), custom_call_target="tpu_custom_call" | custom-call | tf_op jit(solution)/shard_map/pallas_call | solution.py:507
  161.1 1.2 copy.5
Async XLA Ops:
  0.0 1.0 copy-start
